TPU v7x, 32 devices: a whole 2x2x4 slice. The times are simulated.
32 devices in a mesh: rep: 4 (over x, core), row: 4 (over z), col: 2 (over y).
Axes of the slice: x: 2, y: 2, z: 4, core: 2. Of those that a mesh axis runs over, the one named last changes fastest.
Arguments:
- inputs: bfloat16 [4, 128, 6144], P('rep', 'col', 'row'), may hold values from -6 to 6
- w_in: bfloat16 [6144, 24576], P('row', ('rep', 'col')), may hold values from -0.078125 to 0.078125
- w_out: bfloat16 [24576, 6144], P(('rep', 'col'), 'row'), may hold values from -0.0390625 to 0.0390625
- cotangent: bfloat16 [4, 128, 6144], P('rep', 'col', 'row'), may hold values from -1536 to 1536
- counts: int32 [4], replicated, may hold values from 0 to 4, as said below
Outputs:
- block_output: bfloat16 [4, 128, 6144], P('rep', 'col', 'row')
- input_grad: bfloat16 [4, 128, 6144], P('rep', 'col', 'row')
- w_in_grad: float32 [6144, 24576], P('row', ('rep', 'col'))
- w_out_grad: float32 [24576, 6144], P(('rep', 'col'), 'row')
Inputs may be any that keep to these rules, and one draw needn't show every extreme that they name: Replica r completed its first counts[r] micro-batches; at least one replica completed all 4.
All inputs are finite; a program needn't handle non-finite values.
Results may differ from a plain program's by a relative error of at most 0.015.
Values may be sent and summed in bfloat16 or wider, within the bound.
A program may use at most 192 MiB of HBM per device.

v0:
```python
import jax
import jax.numpy as jnp
from jax import lax
from jax.sharding import PartitionSpec as P

MBT = 32
root_coef = 0.7978845608028654
cubic_coef = 0.044715


def gelu_tanh(values):
    inner = root_coef * (values + cubic_coef * values * values * values)
    return 0.5 * values * (1.0 + jnp.tanh(inner))


def gelu_slope(values):
    inner = root_coef * (values + cubic_coef * values * values * values)
    tangent = jnp.tanh(inner)
    return 0.5 * (1.0 + tangent) + 0.5 * values * (1.0 - tangent * tangent) * root_coef * (
        1.0 + 3.0 * cubic_coef * values * values
    )


def right_product(left, right):
    return lax.dot_general(
        left, right, (((1,), (1,)), ((), ())), preferred_element_type=jnp.float32
    )


def first_product(left, right):
    return lax.dot_general(
        left, right, (((0,), (0,)), ((), ())), preferred_element_type=jnp.float32
    )


def body(inputs, w_in, w_out, cotangent, counts):
    rows_local = inputs.shape[1]
    width_local = inputs.shape[2]
    tokens_local = inputs.reshape(rows_local, width_local)
    replicas = lax.axis_size("rep")
    replica_index = lax.axis_index("rep")
    column_index = lax.axis_index("col")
    own_count = jnp.sum(jnp.where(jnp.arange(replicas) == replica_index, counts, 0))
    token_total = (MBT * jnp.sum(counts)).astype(jnp.float32)
    positions = column_index * rows_local + jnp.arange(rows_local, dtype=jnp.int32)
    kept_mask = (positions // MBT < own_count).astype(jnp.float32)
    scaled = (
        cotangent.reshape(rows_local, width_local).astype(jnp.float32)
        * kept_mask[:, None]
        / token_total
    ).astype(jnp.bfloat16)
    tokens_all, scaled_all = (
        lax.all_gather(tokens_local, "col", axis=0, tiled=True),
        lax.all_gather(scaled, "col", axis=0, tiled=True),
    )
    inner_cols = lax.all_gather(w_in, "rep", axis=1, tiled=True)
    outer_rows = lax.all_gather(w_out, "rep", axis=0, tiled=True)
    partial_hidden = jnp.dot(tokens_all, inner_cols, preferred_element_type=jnp.float32)
    hidden = lax.psum_scatter(
        partial_hidden.astype(jnp.bfloat16), "row", scatter_dimension=0, tiled=True
    ).astype(jnp.float32)
    active_share = gelu_tanh(hidden).astype(jnp.bfloat16)
    activated = lax.all_gather(active_share, "row", axis=0, tiled=True)
    output_terms = jnp.dot(activated, outer_rows, preferred_element_type=jnp.float32)
    output_local = lax.psum_scatter(
        output_terms.astype(jnp.bfloat16), "col", scatter_dimension=0, tiled=True
    ).astype(jnp.float32)
    block_output = (tokens_local.astype(jnp.float32) + output_local).astype(jnp.bfloat16)
    slope_terms = right_product(scaled_all, outer_rows)
    slope_sum = lax.psum_scatter(
        slope_terms.astype(jnp.bfloat16), "row", scatter_dimension=0, tiled=True
    ).astype(jnp.float32)
    grad_share = (slope_sum * gelu_slope(hidden)).astype(jnp.bfloat16)
    hidden_grad = lax.all_gather(grad_share, "row", axis=0, tiled=True)
    back_terms = right_product(hidden_grad, inner_cols)
    back_local = lax.psum_scatter(
        back_terms.astype(jnp.bfloat16), "col", scatter_dimension=0, tiled=True
    ).astype(jnp.float32)
    input_grad = (scaled.astype(jnp.float32) + back_local).astype(jnp.bfloat16)
    token_reps, scaled_reps = (
        lax.all_gather(tokens_all, "rep", axis=0, tiled=True),
        lax.all_gather(scaled_all, "rep", axis=0, tiled=True),
    )
    hidden_reps, active_reps = (
        lax.all_to_all(hidden_grad, "rep", split_axis=1, concat_axis=0, tiled=True),
        lax.all_to_all(activated, "rep", split_axis=1, concat_axis=0, tiled=True),
    )
    w_in_grad = first_product(token_reps, hidden_reps)
    w_out_grad = first_product(active_reps, scaled_reps)
    return (
        block_output.reshape(1, rows_local, width_local),
        input_grad.reshape(1, rows_local, width_local),
        w_in_grad,
        w_out_grad,
    )


def solution(mesh):
    placed = (
        P("rep", "col", "row"),
        P("row", ("rep", "col")),
        P(("rep", "col"), "row"),
        P("rep", "col", "row"),
        P(),
    )
    return jax.shard_map(
        body,
        mesh=mesh,
        in_specs=placed,
        out_specs=(
            P("rep", "col", "row"),
            P("rep", "col", "row"),
            P("row", ("rep", "col")),
            P(("rep", "col"), "row"),
        ),
        check_vma=False,
    )
```

profile of v0, /device:TPU:0, one launch (start us, length us, event | category | flops | bytes accessed | tf_op | source)
XLA Modules:
  0.0 861.8 jit_solution(15907317632032920485)
XLA Ops:
  8.8 8.5 all-gather
  17.4 222.1 %all-gather.9.cloned.1.call-done = bf16[1536,12288]{1,0:T(8,128)(2,1)} async-done(((bf16[1536,3072]{1,0:T(8,128)(2,1)}), bf16[1536,12288]{1,0:T(8,128)(2,1)}) %all-gather.9.cloned.1.call-update) | async-done | bytes 37748752 | tf_op jit(solution)/shard_map/all_gather | solution.py:56
  239.5 20.2 %convolution_convert_fusion.1 = bf16[128,12288]{1,0:T(8,128)(2,1)} fusion(bf16[1536,12288]{1,0:T(8,128)(2,1)} %all-gather.9.cloned.1.call-done, bf16[1,128,1536]{2,1,0:T(8,128)(2,1)S(1)} %all-gather), kind=kOutput, calls=%fused_computation.1 | convolution fusion | flops 4833411072 | bytes 41287680 | tf_op jit(solution)/shard_map/dot_general | solution.py:58
  262.4 7.7 all_gather.28
  270.1 198.2 %all-gather.13.cloned.1.call-done = bf16[12288,1536]{1,0:T(8,128)(2,1)} async-done(((bf16[3072,1536]{1,0:T(8,128)(2,1)}), bf16[12288,1536]{1,0:T(8,128)(2,1)}) %all-gather.13.cloned.1.call-update) | async-done | bytes 37748752 | tf_op jit(solution)/shard_map/all_gather | solution.py:57
  468.3 19.7 %convolution_convert_fusion = bf16[128,12288]{1,0:T(8,128)(2,1)} fusion(bf16[128,1536]{1,0:T(8,128)(2,1)S(1)} %all_gather.28, bf16[12288,1536]{1,0:T(8,128)(2,1)} %all-gather.13.cloned.1.call-done), kind=kOutput, calls=%fused_computation | convolution fusion | flops 4833411072 | bytes 41287680 | tf_op jit(solution)/shard_map/dot_general | solution.py:25
  488.1 43.5 %reduce-scatter.5.cloned.1.call-done = bf16[32,12288]{1,0:T(8,128)(2,1)} async-done(((bf16[128,12288]{1,0:T(8,128)(2,1)}), bf16[32,12288]{1,0:T(8,128)(2,1)}) %reduce-scatter.5.cloned.1.call-update) | async-done | bytes 786448 | tf_op jit(solution)/shard_map/reduce_scatter | solution.py:59
  531.6 63.0 %reduce-scatter.9.cloned.1.call-done = bf16[32,12288]{1,0:T(8,128)(2,1)} async-done(((bf16[128,12288]{1,0:T(8,128)(2,1)}), bf16[32,12288]{1,0:T(8,128)(2,1)}) %reduce-scatter.9.cloned.1.call-update) | async-done | bytes 786448 | tf_op jit(solution)/shard_map/reduce_scatter | solution.py:70
  594.6 3.7 fusion.7
  599.0 62.9 %all-gather.11.cloned.1.call-done = bf16[128,12288]{1,0:T(8,128)(2,1)} async-done(((bf16[32,12288]{1,0:T(8,128)(2,1)}), bf16[128,12288]{1,0:T(8,128)(2,1)}) %all-gather.11.cloned.1.call-update) | async-done | bytes 3145744 | tf_op jit(solution)/shard_map/all_gather | solution.py:63
  661.9 16.8 %convolution_convert_fusion.3 = bf16[128,1536]{1,0:T(8,128)(2,1)} fusion(bf16[128,12288]{1,0:T(8,128)(2,1)} %all-gather.11.cloned.1.call-done, bf16[12288,1536]{1,0:T(8,128)(2,1)} %all-gather.13.cloned.1.call-done), kind=kOutput, calls=%fused_computation.13 | convolution fusion | flops 4832034816 | bytes 41287680 | tf_op jit(solution)/shard_map/dot_general | solution.py:64
  678.9 47.1 %all-gather.15.cloned.1.call-done = bf16[128,12288]{1,0:T(8,128)(2,1)} async-done(((bf16[32,12288]{1,0:T(8,128)(2,1)}), bf16[128,12288]{1,0:T(8,128)(2,1)}) %all-gather.15.cloned.1.call-update) | async-done | bytes 3145744 | tf_op jit(solution)/shard_map/all_gather | solution.py:74
  726.0 23.0 %convolution_convert_fusion.2 = bf16[128,1536]{1,0:T(8,128)(2,1)} fusion(bf16[128,12288]{1,0:T(8,128)(2,1)} %all-gather.15.cloned.1.call-done, bf16[1536,12288]{1,0:T(8,128)(2,1)} %all-gather.9.cloned.1.call-done), kind=kOutput, calls=%fused_computation.12 | convolution fusion | flops 4832034816 | bytes 41287680 | tf_op jit(solution)/shard_map/dot_general | solution.py:25
  749.8 1.9 copy.18
  751.7 4.9 all-to-all-start
  757.2 1.9 copy.17
  759.2 42.9 %all-to-all-done = bf16[128,4,3072]{2,0,1:T(8,128)(2,1)} async-done(((bf16[128,4,3072]{2,0,1:T(8,128)(2,1)}), bf16[128,4,3072]{2,0,1:T(8,128)(2,1)}, u32[]{:S(2)}, u32[]{:S(2)}) %all-to-all-start) | async-done | bytes 3145760 | tf_op jit(solution)/shard_map/all_to_all | solution.py:85
  802.0 3.8 all-to-all-start.1
  805.9 1.7 fusion.17
  807.6 1.7 fusion.16
  809.3 11.4 %convolution_bitcast_fusion = f32[1536,3072]{0,1:T(8,128)} fusion(bf16[512,3072]{1,0:T(8,128)(2,1)} %bitcast.6, bf16[1,512,1536]{2,1,0:T(8,128)(2,1)} %all-gather.19.cloned.1.call-done), kind=kOutput, calls=%fused_computation.2 | convolution fusion | flops 4831838208 | bytes 23592960 | tf_op jit(solution)/shard_map/dot_general | solution.py:31
  820.7 18.6 %copy.12 = f32[1536,3072]{1,0:T(8,128)} copy(f32[1536,3072]{0,1:T(8,128)} %convolution_bitcast_fusion) | data formatting | bytes 37748736
  839.3 4.7 all-to-all-done.1
  844.1 10.9 %fusion.19 = f32[3072,1536]{1,0:T(8,128)} fusion(bf16[512,3072]{1,0:T(8,128)(2,1)S(1)} %bitcast.48, bf16[512,1536]{1,0:T(8,128)(2,1)} %all-gather.17.cloned.1.call-done), kind=kOutput, calls=%fused_computation.42 | convolution fusion | flops 4831838208 | bytes 23592960 | tf_op jit(solution)/shard_map/dot_general | solution.py:31
  (45 shorter events, 6.0 us)
Async XLA Ops:
  7.2 232.3 %all-gather.9.cloned.1.call-start = ((), (), s32[]{:S(2)}) async-start(), calls=%async_computation.6 | async-start | bytes 47185920 | tf_op jit(solution)/shard_map/all_gather | solution.py:56
  7.9 0.9 copy-start.6
  7.9 460.3 %all-gather.13.cloned.1.call-start = ((), (), s32[]{:S(2)}) async-start(), calls=%async_computation.9 | async-start | bytes 47185920 | tf_op jit(solution)/shard_map/all_gather | solution.py:57
  8.7 522.9 %reduce-scatter.5.cloned.1.call-start = ((), (), s32[]{:S(2)}) async-start(), calls=%async_computation.7 | async-start | bytes 3932160 | tf_op jit(solution)/shard_map/reduce_scatter | solution.py:59
  17.4 242.3 %copy-start.2 = (bf16[1,128,1536]{2,1,0:T(8,128)(2,1)}, bf16[1,128,1536]{2,1,0:T(8,128)(2,1)S(1)}, u32[]{:S(2)}) copy-start(bf16[1,128,1536]{2,1,0:T(8,128)(2,1)S(1)} %all-gather) | copy-start | bytes 1179652
  259.6 0.7 copy-start.8
  259.6 2.6 copy-start.4
  259.7 335.0 %reduce-scatter.9.cloned.1.call-start = ((), (), s32[]{:S(2)}) async-start(), calls=%async_computation.11 | async-start | bytes 3932160 | tf_op jit(solution)/shard_map/reduce_scatter | solution.py:70
  270.1 217.9 %copy-start.3 = (bf16[128,1536]{1,0:T(8,128)(2,1)}, bf16[128,1536]{1,0:T(8,128)(2,1)S(1)}, u32[]{:S(2)}) copy-start(bf16[128,1536]{1,0:T(8,128)(2,1)S(1)} %all_gather.28) | copy-start | bytes 1179652
  488.0 173.8 %all-gather.11.cloned.1.call-start = ((), (), s32[]{:S(2)}) async-start(), calls=%async_computation.8 | async-start | bytes 3932160 | tf_op jit(solution)/shard_map/all_gather | solution.py:63
  598.3 127.6 %all-gather.15.cloned.1.call-start = ((), (), s32[]{:S(2)}) async-start(), calls=%async_computation.12 | async-start | bytes 3932160 | tf_op jit(solution)/shard_map/all_gather | solution.py:74
  598.9 207.0 %reduce-scatter.7.cloned.1.call-start = ((), (), s32[]{:S(2)}) async-start(), calls=%async_computation.10 | async-start | bytes 589824 | tf_op jit(solution)/shard_map/reduce_scatter | solution.py:65
  678.7 128.9 %reduce-scatter.11.cloned.1.call-start = ((), (), s32[]{:S(2)}) async-start(), calls=%async_computation.13 | async-start | bytes 589824 | tf_op jit(solution)/shard_map/reduce_scatter | solution.py:76
  726.0 23.8 %copy-start = (bf16[128,12288]{1,0:T(8,128)(2,1)S(1)}, bf16[128,12288]{1,0:T(8,128)(2,1)}, u32[]{:S(2)}) copy-start(bf16[128,12288]{1,0:T(8,128)(2,1)} %all-gather.15.cloned.1.call-done) | copy-start | bytes 9437188
  749.0 60.3 %all-gather.19.cloned.1.call-start = ((), (), s32[]{:S(2)}) async-start(), calls=%async_computation.15 | async-start | bytes 1966080 | tf_op jit(solution)/shard_map/all_gather | solution.py:81
  751.7 5.5 copy-start.1
  751.7 50.3 %all-to-all-start = ((bf16[128,4,3072]{2,0,1:T(8,128)(2,1)}), bf16[128,4,3072]{2,0,1:T(8,128)(2,1)}, u32[]{:S(2)}, u32[]{:S(2)}) async-start(bf16[128,4,3072]{2,0,1:T(8,128)(2,1)} %bitcast.47), calls=%async_computation.4 | async-start | bytes 6291456 | tf_op jit(solution)/shard_map/all_to_all | solution.py:85
  756.6 82.7 %all-gather.17.cloned.1.call-start = ((), (), s32[]{:S(2)}) async-start(), calls=%async_computation.14 | async-start | bytes 1966080 | tf_op jit(solution)/shard_map/all_gather | solution.py:82
  802.0 3.9 copy-start.7
  802.0 5.5 copy-start.5
  802.0 42.0 %all-to-all-start.1 = ((bf16[128,4,3072]{2,0,1:T(8,128)(2,1)}), bf16[128,4,3072]{2,0,1:T(8,128)(2,1)S(1)}, u32[]{:S(2)}, u32[]{:S(2)}) async-start(bf16[128,4,3072]{2,0,1:T(8,128)(2,1)} %bitcast.46), calls=%async_computation.5 | async-start | bytes 6291456 | tf_op jit(solution)/shard_map/all_to_all | solution.py:86
Sparse Core Ops, SparseCore 0:
  9.5 229.8 all-gather.8
  241.0 227.1 all-gather.12
  471.1 60.4 reduce-scatter.4
  534.3 60.2 reduce-scatter.8
  598.5 63.3 all-gather.10
  663.9 62.0 all-gather.14
  728.8 11.8 reduce-scatter.6
  749.1 11.8 reduce-scatter.10
  762.6 28.1 all-gather.18
  792.2 21.0 all-gather.16
where the time goes:
time: 863 us; the launch traced here: 862 us
  waiting for transfers between devices  688 us (80%)
  matrix products  102 us (12%)
  local copies, waits for them, and re-layouts  23.2 us (3%)
  blocking collectives  16.2 us (2%)
  between operations  14.9 us (2%)
  starting transfers between devices  9.32 us (1%)
    all_gather x1, waiting for transfers between devices, body(): inner_cols = lax.all_gather(w_in, 'rep', axis=1, tiled=True)  222 us
    all_gather x1, waiting for transfers between devices, body(): outer_rows = lax.all_gather(w_out, 'rep', axis=0, tiled=True)  198 us
    reduce_scatter x1, waiting for transfers between devices, body(): lax.psum_scatter(slope_terms.astype(jnp.bfloat16), 'row', scatter_dimensi...  63 us
    all_gather x1, waiting for transfers between devices, body(): activated = lax.all_gather(active_share, 'row', axis=0, tiled=True)  62.9 us
    all_gather x1, waiting for transfers between devices, body(): hidden_grad = lax.all_gather(grad_share, 'row', axis=0, tiled=True)  47.1 us
    reduce_scatter x1, waiting for transfers between devices, body(): lax.psum_scatter(partial_hidden.astype(jnp.bfloat16), 'row', scatter_dime...  43.5 us
    all_to_all x1, waiting for transfers between devices, body(): lax.all_to_all(hidden_grad, 'rep', split_axis=1, concat_axis=0, tiled=True)  42.9 us
    dot_general x2, matrix products, right_product(): lax.dot_general(left, right, (((1,), (1,)), ((), ())), preferred_element_...  42.8 us
  transfers between devices with their start and end apart: 12, of which 8 were waited for; matrix products, arithmetic and copies ran while one was open for 14% of the time, Pallas kernels for 0%

commit v1 on v0

--- a/solution.py
+++ b/solution.py
@@ -71,7 +71,24 @@
         slope_terms.astype(jnp.bfloat16), "row", scatter_dimension=0, tiled=True
     ).astype(jnp.float32)
     grad_share = (slope_sum * gelu_slope(hidden)).astype(jnp.bfloat16)
-    hidden_grad = lax.all_gather(grad_share, "row", axis=0, tiled=True)
+    length, index, rows = (lax.axis_size("row"), lax.axis_index("row"), grad_share.shape[0])
+    ahead = [(i, (i + 1) % length) for i in range(length)]
+    left_2 = [(i, (i - 1) % length) for i in range(length)]
+    out = jnp.zeros(
+        (*grad_share.shape[:0], length * rows, *grad_share.shape[0 + 1 :]), grad_share.dtype
+    )
+    out = lax.dynamic_update_slice_in_dim(out, grad_share, index * rows, axis=0)
+    from_left = from_right = grad_share
+    middle = length // 2
+    for hop in range(1, middle + 1):
+        from_left = lax.ppermute(from_left, "row", ahead)
+        out = lax.dynamic_update_slice_in_dim(out, from_left, (index - hop) % length * rows, axis=0)
+        if hop < length - middle:
+            from_right = lax.ppermute(from_right, "row", left_2)
+            out = lax.dynamic_update_slice_in_dim(
+                out, from_right, (index + hop) % length * rows, axis=0
+            )
+    hidden_grad = out
     back_terms = right_product(hidden_grad, inner_cols)
     back_local = lax.psum_scatter(
         back_terms.astype(jnp.bfloat16), "col", scatter_dimension=0, tiled=True

time: 863 us -> 933 us (1.081)
  local copies, waits for them, and re-layouts: 23.2 us -> 162 us
  waiting for transfers between devices: 688 us -> 592 us
  starting transfers between devices: 9.32 us -> 39.1 us
    dynamic_update_slice x0 -> x4, local copies, waits for them, and re-layouts: none -> 122 us  [the longest x2 63.7 us: body(): lax.dynamic_update_slice_in_dim(out, from_left, (index - hop) % length *...]
    all_gather x1, waiting for transfers between devices: 62.9 us -> 0.02 us  [body(): activated = lax.all_gather(active_share, 'row', axis=0, tiled=True)]
    all_gather x1 -> x0, waiting for transfers between devices: 47.1 us -> none  [body(): hidden_grad = lax.all_gather(grad_share, 'row', axis=0, tiled=True)]
    ppermute x0 -> x3, starting transfers between devices: none -> 30 us  [the longest x2 27.1 us: body(): from_left = lax.ppermute(from_left, 'row', ahead)]
    ppermute x0 -> x3, waiting for transfers between devices: none -> 28.7 us  [the longest x2 28.7 us: body(): from_left = lax.ppermute(from_left, 'row', ahead)]
    all_to_all x1, waiting for transfers between devices: 42.9 us -> 26.2 us  [body(): lax.all_to_all(hidden_grad, 'rep', split_axis=1, concat_axis=0, tiled=True)]
    unnamed x19 -> x17, local copies, waits for them, and re-layouts: 19.4 us -> 19.4 us
  transfers between devices with their start and end apart: 12 -> 14, of which waited for: 8 -> 7; matrix products, arithmetic and copies ran while one was open for 14% -> 27% of each run, Pallas kernels for 0% -> 0%
where the time goes in v1:
time: 933 us; the launch traced here: 929 us
  waiting for transfers between devices  592 us (63%)
  local copies, waits for them, and re-layouts  162 us (17%)
  matrix products  97.8 us (10%)
  starting transfers between devices  39.1 us (4%)
  blocking collectives  16.2 us (2%)
  between operations  14.7 us (2%)
    all_gather x1, waiting for transfers between devices, body(): inner_cols = lax.all_gather(w_in, 'rep', axis=1, tiled=True)  222 us
    all_gather x1, waiting for transfers between devices, body(): outer_rows = lax.all_gather(w_out, 'rep', axis=0, tiled=True)  198 us
    dynamic_update_slice x2, local copies, waits for them, and re-layouts, body(): lax.dynamic_update_slice_in_dim(out, from_left, (index - hop) % length *...  63.7 us
    reduce_scatter x1, waiting for transfers between devices, body(): lax.psum_scatter(slope_terms.astype(jnp.bfloat16), 'row', scatter_dimensi...  63.1 us
    reduce_scatter x1, waiting for transfers between devices, body(): lax.psum_scatter(partial_hidden.astype(jnp.bfloat16), 'row', scatter_dime...  43.5 us
    dot_general x2, matrix products, right_product(): lax.dot_general(left, right, (((1,), (1,)), ((), ())), preferred_element_...  38.9 us
    dynamic_update_slice x1, local copies, waits for them, and re-layouts, body(): lax.dynamic_update_slice_in_dim(out, from_right, (index + hop) % length *...  31.8 us
    ppermute x2, waiting for transfers between devices, body(): from_left = lax.ppermute(from_left, 'row', ahead)  28.7 us
  transfers between devices with their start and end apart: 14, of which 7 were waited for; matrix products, arithmetic and copies ran while one was open for 27% of the time, Pallas kernels for 0%

profile of v1, /device:TPU:0, one launch (start us, length us, event | category | flops | bytes accessed | tf_op | source)
XLA Modules:
  0.0 929.4 jit_solution(12833547399066021182)
XLA Ops:
  8.8 8.5 all-gather
  17.4 222.1 %all-gather.8.cloned.1.call-done = bf16[1536,12288]{1,0:T(8,128)(2,1)} async-done(((bf16[1536,3072]{1,0:T(8,128)(2,1)}), bf16[1536,12288]{1,0:T(8,128)(2,1)}) %all-gather.8.cloned.1.call-update) | async-done | bytes 37748752 | tf_op jit(solution)/shard_map/all_gather | solution.py:56
  239.5 20.2 %convolution_convert_fusion.1 = bf16[128,12288]{1,0:T(8,128)(2,1)} fusion(bf16[1536,12288]{1,0:T(8,128)(2,1)} %all-gather.8.cloned.1.call-done, bf16[1,128,1536]{2,1,0:T(8,128)(2,1)S(1)} %all-gather), kind=kOutput, calls=%fused_computation.1 | convolution fusion | flops 4833411072 | bytes 41287680 | tf_op jit(solution)/shard_map/dot_general | solution.py:58
  262.4 7.7 all_gather.25
  270.1 198.2 %all-gather.12.cloned.1.call-done = bf16[12288,1536]{1,0:T(8,128)(2,1)} async-done(((bf16[3072,1536]{1,0:T(8,128)(2,1)}), bf16[12288,1536]{1,0:T(8,128)(2,1)}) %all-gather.12.cloned.1.call-update) | async-done | bytes 37748752 | tf_op jit(solution)/shard_map/all_gather | solution.py:57
  468.3 19.8 %convolution_convert_fusion = bf16[128,12288]{1,0:T(8,128)(2,1)} fusion(bf16[128,1536]{1,0:T(8,128)(2,1)S(1)} %all_gather.25, bf16[12288,1536]{1,0:T(8,128)(2,1)} %all-gather.12.cloned.1.call-done), kind=kOutput, calls=%fused_computation | convolution fusion | flops 4833411072 | bytes 41287680 | tf_op jit(solution)/shard_map/dot_general | solution.py:25
  488.1 43.5 %reduce-scatter.5.cloned.1.call-done = bf16[32,12288]{1,0:T(8,128)(2,1)} async-done(((bf16[128,12288]{1,0:T(8,128)(2,1)}), bf16[32,12288]{1,0:T(8,128)(2,1)}) %reduce-scatter.5.cloned.1.call-update) | async-done | bytes 786448 | tf_op jit(solution)/shard_map/reduce_scatter | solution.py:59
  531.6 63.1 %reduce-scatter.9.cloned.1.call-done = bf16[32,12288]{1,0:T(8,128)(2,1)} async-done(((bf16[128,12288]{1,0:T(8,128)(2,1)}), bf16[32,12288]{1,0:T(8,128)(2,1)}) %reduce-scatter.9.cloned.1.call-update) | async-done | bytes 786448 | tf_op jit(solution)/shard_map/reduce_scatter | solution.py:70
  602.3 28.7 %collective-permute-done = bf16[32,12288]{1,0:T(8,128)(2,1)} collective-permute-done((bf16[32,12288]{1,0:T(8,128)(2,1)}, bf16[32,12288]{1,0:T(8,128)(2,1)}, u32[]{:S(2)}, u32[]{:S(2)}) %collective-permute-start) | collective-permute-done | bytes 786464 | tf_op jit(solution)/shard_map/ppermute | solution.py:84
  631.0 26.1 %collective-permute-start.2 = (bf16[32,12288]{1,0:T(8,128)(2,1)}, bf16[32,12288]{1,0:T(8,128)(2,1)}, u32[]{:S(2)}, u32[]{:S(2)}) collective-permute-start(bf16[32,12288]{1,0:T(8,128)(2,1)} %collective-permute-done), channel_id=1, source_target_pairs={{0,2},{2,4},{4,6},{6,0},{1,3},{3,5},{5,7},{7,1},{8,10},{10,12},{12... | collective-permute-start | bytes 2359304 | tf_op jit(solution)/shard_map/ppermute | solution.py:84
  661.8 26.8 %dynamic_update_slice.12 = bf16[128,12288]{0,1:T(8,128)(2,1)} dynamic-update-slice(bf16[128,12288]{0,1:T(8,128)(2,1)} %broadcast_in_dim.9, bf16[32,12288]{0,1:T(8,128)(2,1)S(1)} %copy.12, s32[]{:T(128)S(6)} %select_n.42, s32[]{:T(128)} %constant.58.clone.1) | dynamic-update-slice | bytes 1572868 | tf_op jit(solution)/shard_map/dynamic_update_slice | solution.py:80
  691.5 31.8 %dynamic_update_slice.13 = bf16[128,12288]{0,1:T(8,128)(2,1)} dynamic-update-slice(bf16[128,12288]{0,1:T(8,128)(2,1)} %dynamic_update_slice.12, bf16[32,12288]{0,1:T(8,128)(2,1)S(1)} %copy.13, s32[]{:T(128)S(6)} %select_n.44, s32[]{:T(128)} %constant.58.clone.1) | dynamic-update-slice | bytes 1572868 | tf_op jit(solution)/shard_map/dynamic_update_slice | solution.py:85
  726.2 31.8 %dynamic_update_slice.14 = bf16[128,12288]{0,1:T(8,128)(2,1)} dynamic-update-slice(bf16[128,12288]{0,1:T(8,128)(2,1)} %dynamic_update_slice.13, bf16[32,12288]{0,1:T(8,128)(2,1)S(1)} %copy.14, s32[]{:T(128)S(6)} %select_n.46, s32[]{:T(128)} %constant.58.clone.1) | dynamic-update-slice | bytes 1572868 | tf_op jit(solution)/shard_map/dynamic_update_slice | solution.py:88
  760.9 31.8 %dynamic_update_slice.15 = bf16[128,12288]{0,1:T(8,128)(2,1)} dynamic-update-slice(bf16[128,12288]{0,1:T(8,128)(2,1)} %dynamic_update_slice.14, bf16[32,12288]{0,1:T(8,128)(2,1)S(1)} %copy.15, s32[]{:T(128)S(6)} %select_n.48, s32[]{:T(128)} %constant.58.clone.1) | dynamic-update-slice | bytes 1572868 | tf_op jit(solution)/shard_map/dynamic_update_slice | solution.py:85
  792.8 19.2 %convolution_convert_fusion.2 = bf16[128,1536]{1,0:T(8,128)(2,1)} fusion(bf16[128,12288]{0,1:T(8,128)(2,1)} %dynamic_update_slice.15, bf16[1536,12288]{1,0:T(8,128)(2,1)} %all-gather.8.cloned.1.call-done), kind=kOutput, calls=%fused_computation.11 | convolution fusion | flops 4832034816 | bytes 41287680 | tf_op jit(solution)/shard_map/dot_general | solution.py:25
  812.7 4.7 all-to-all-start
  817.5 16.4 %convolution_convert_fusion.3 = bf16[128,1536]{1,0:T(8,128)(2,1)} fusion(bf16[128,12288]{1,0:T(8,128)(2,1)} %all-gather.10.cloned.1.call-done, bf16[12288,1536]{1,0:T(8,128)(2,1)} %all-gather.12.cloned.1.call-done), kind=kOutput, calls=%fused_computation.12 | convolution fusion | flops 4832034816 | bytes 41287680 | tf_op jit(solution)/shard_map/dot_general | solution.py:64
  836.5 26.2 %all-to-all-done = bf16[128,4,3072]{0,2,1:T(8,128)(2,1)} async-done(((bf16[128,4,3072]{0,2,1:T(8,128)(2,1)}), bf16[128,4,3072]{0,2,1:T(8,128)(2,1)}, u32[]{:S(2)}, u32[]{:S(2)}) %all-to-all-start) | async-done | bytes 3145760 | tf_op jit(solution)/shard_map/all_to_all | solution.py:102
  862.8 4.1 all-to-all-start.1
  868.6 4.6 copy.16
  873.3 11.4 %convolution_bitcast_fusion = f32[1536,3072]{0,1:T(8,128)} fusion(bf16[512,3072]{1,0:T(8,128)(2,1)} %bitcast.43, bf16[1,512,1536]{2,1,0:T(8,128)(2,1)} %all-gather.16.cloned.1.call-done), kind=kOutput, calls=%fused_computation.2 | convolution fusion | flops 4831838208 | bytes 23592960 | tf_op jit(solution)/shard_map/dot_general | solution.py:31
  884.7 18.7 %copy.18 = f32[1536,3072]{1,0:T(8,128)} copy(f32[1536,3072]{0,1:T(8,128)} %convolution_bitcast_fusion) | data formatting | bytes 37748736
  905.0 6.9 all-to-all-done.1
  911.9 10.9 %fusion.19 = f32[3072,1536]{1,0:T(8,128)} fusion(bf16[512,3072]{1,0:T(8,128)(2,1)S(1)} %bitcast.42, bf16[512,1536]{1,0:T(8,128)(2,1)} %all-gather.14.cloned.1.call-done), kind=kOutput, calls=%fused_computation.41 | convolution fusion | flops 4831838208 | bytes 23592960 | tf_op jit(solution)/shard_map/dot_general | solution.py:31
  (55 shorter events, 31.6 us)
Async XLA Ops:
  7.2 232.3 %all-gather.8.cloned.1.call-start = ((), (), s32[]{:S(2)}) async-start(), calls=%async_computation.6 | async-start | bytes 47185920 | tf_op jit(solution)/shard_map/all_gather | solution.py:56
  7.9 0.9 copy-start.5
  7.9 460.3 %all-gather.12.cloned.1.call-start = ((), (), s32[]{:S(2)}) async-start(), calls=%async_computation.9 | async-start | bytes 47185920 | tf_op jit(solution)/shard_map/all_gather | solution.py:57
  8.7 522.9 %reduce-scatter.5.cloned.1.call-start = ((), (), s32[]{:S(2)}) async-start(), calls=%async_computation.7 | async-start | bytes 3932160 | tf_op jit(solution)/shard_map/reduce_scatter | solution.py:59
  17.4 242.3 %copy-start.1 = (bf16[1,128,1536]{2,1,0:T(8,128)(2,1)}, bf16[1,128,1536]{2,1,0:T(8,128)(2,1)S(1)}, u32[]{:S(2)}) copy-start(bf16[1,128,1536]{2,1,0:T(8,128)(2,1)S(1)} %all-gather) | copy-start | bytes 1179652
  259.6 0.7 copy-start.7
  259.6 2.6 copy-start.3
  259.7 335.0 %reduce-scatter.9.cloned.1.call-start = ((), (), s32[]{:S(2)}) async-start(), calls=%async_computation.11 | async-start | bytes 3932160 | tf_op jit(solution)/shard_map/reduce_scatter | solution.py:70
  270.1 218.0 %copy-start.2 = (bf16[128,1536]{1,0:T(8,128)(2,1)}, bf16[128,1536]{1,0:T(8,128)(2,1)S(1)}, u32[]{:S(2)}) copy-start(bf16[128,1536]{1,0:T(8,128)(2,1)S(1)} %all_gather.25) | copy-start | bytes 1179652
  488.0 329.4 %all-gather.10.cloned.1.call-start = ((), (), s32[]{:S(2)}) async-start(), calls=%async_computation.8 | async-start | bytes 3932160 | tf_op jit(solution)/shard_map/all_gather | solution.py:63
  598.3 268.5 %reduce-scatter.11.cloned.1.call-start = ((), (), s32[]{:S(2)}) async-start(), calls=%async_computation.12 | async-start | bytes 589824 | tf_op jit(solution)/shard_map/reduce_scatter | solution.py:93
  598.4 32.6 %collective-permute-start = (bf16[32,12288]{1,0:T(8,128)(2,1)}, bf16[32,12288]{1,0:T(8,128)(2,1)}, u32[]{:S(2)}, u32[]{:S(2)}) collective-permute-start(bf16[32,12288]{1,0:T(8,128)(2,1)} %get-tuple-element.18), channel_id=1, source_target_pairs={{0,2},{2,4},{4,6},{6,0},{1,3},{3,5},{5,7},{7,1},{8,10},{10,12},{12... | collective-permute-start | bytes 2359304 | tf_op jit(solution)/shard_map/ppermute | solution.py:84
  599.3 124.0 %collective-permute-start.1 = (bf16[32,12288]{1,0:T(8,128)(2,1)}, bf16[32,12288]{1,0:T(8,128)(2,1)}, u32[]{:S(2)}, u32[]{:S(2)}) collective-permute-start(bf16[32,12288]{1,0:T(8,128)(2,1)} %get-tuple-element.18), channel_id=1, source_target_pairs={{0,6},{2,0},{4,2},{6,4},{1,7},{3,1},{5,3},{7,5},{8,14},{10,8},{12,... | collective-permute-start | bytes 2359304 | tf_op jit(solution)/shard_map/ppermute | solution.py:87
  631.0 127.1 %collective-permute-start.2 = (bf16[32,12288]{1,0:T(8,128)(2,1)}, bf16[32,12288]{1,0:T(8,128)(2,1)}, u32[]{:S(2)}, u32[]{:S(2)}) collective-permute-start(bf16[32,12288]{1,0:T(8,128)(2,1)} %collective-permute-done), channel_id=1, source_target_pairs={{0,2},{2,4},{4,6},{6,0},{1,3},{3,5},{5,7},{7,1},{8,10},{10,12},{12... | collective-permute-start | bytes 2359304 | tf_op jit(solution)/shard_map/ppermute | solution.py:84
  812.0 61.3 %all-gather.16.cloned.1.call-start = ((), (), s32[]{:S(2)}) async-start(), calls=%async_computation.14 | async-start | bytes 1966080 | tf_op jit(solution)/shard_map/all_gather | solution.py:98
  812.7 50.1 %all-to-all-start = ((bf16[128,4,3072]{0,2,1:T(8,128)(2,1)}), bf16[128,4,3072]{0,2,1:T(8,128)(2,1)}, u32[]{:S(2)}, u32[]{:S(2)}) async-start(bf16[128,4,3072]{0,2,1:T(8,128)(2,1)} %bitcast.5), calls=%async_computation.4 | async-start | bytes 6291456 | tf_op jit(solution)/shard_map/all_to_all | solution.py:102
  817.4 86.0 %reduce-scatter.7.cloned.1.call-start = ((), (), s32[]{:S(2)}) async-start(), calls=%async_computation.10 | async-start | bytes 589824 | tf_op jit(solution)/shard_map/reduce_scatter | solution.py:65
  817.5 17.2 %copy-start = (bf16[128,12288]{1,0:T(8,128)(2,1)S(1)}, bf16[128,12288]{1,0:T(8,128)(2,1)}, u32[]{:S(2)}) copy-start(bf16[128,12288]{1,0:T(8,128)(2,1)} %all-gather.10.cloned.1.call-done) | copy-start | bytes 9437188
  833.9 71.1 %all-gather.14.cloned.1.call-start = ((), (), s32[]{:S(2)}) async-start(), calls=%async_computation.13 | async-start | bytes 1966080 | tf_op jit(solution)/shard_map/all_gather | solution.py:99
  862.8 4.1 copy-start.4
  862.8 49.1 %all-to-all-start.1 = ((bf16[128,4,3072]{2,0,1:T(8,128)(2,1)}), bf16[128,4,3072]{2,0,1:T(8,128)(2,1)S(1)}, u32[]{:S(2)}, u32[]{:S(2)}) async-start(bf16[128,4,3072]{2,0,1:T(8,128)(2,1)} %bitcast.41), calls=%async_computation.5 | async-start | bytes 6291456 | tf_op jit(solution)/shard_map/all_to_all | solution.py:103
  884.7 18.7 %copy-start.6 = (bf16[1,64,1536]{2,1,0:T(8,128)(2,1)S(1)}, bf16[1,64,1536]{2,1,0:T(8,128)(2,1)}, u32[]{:S(2)}) copy-start(bf16[1,64,1536]{2,1,0:T(8,128)(2,1)} %param.5) | copy-start | bytes 589828
Sparse Core Ops, SparseCore 0:
  9.5 229.8 all-gather.7
  241.0 227.1 all-gather.11
  471.1 60.3 reduce-scatter.4
  534.3 60.3 reduce-scatter.8
  598.5 105.4 all-gather.9
  812.1 14.2 reduce-scatter.10
  827.9 28.1 all-gather.15
  858.4 12.2 reduce-scatter.6
  872.2 28.1 all-gather.13
